TPU v7x, 512 devices: a whole 4x8x8 slice. The times are simulated.
512 devices in a mesh: ctx: 64 (over x, y, core), heads: 8 (over z).
Axes of the slice: x: 4, y: 8, z: 8, core: 2. Of those that a mesh axis runs over, the one named last changes fastest.
Arguments:
- ssm_input: bfloat16 [12288, 8192], P('ctx', 'heads'), may hold values from -36 to 36
- gate_input: bfloat16 [12288, 8192], P('ctx', 'heads'), may hold values from -6 to 6
- write_proj: bfloat16 [12288, 128], P('ctx'), may hold values from -0.5 to 0.5
- read_proj: bfloat16 [12288, 128], P('ctx'), may hold values from -0.5 to 0.5
- log_decay: float32 [12288, 128], P('ctx', 'heads'), may hold values from -0.75 to 0, as said below
- skip_gain: float32 [128], P('heads'), may hold values from 0.5 to 2
- norm_gain: float32 [8192], P('heads'), may hold values from 0.1 to 1.9
- query_rows: bfloat16 [12288, 4096], P('ctx', 'heads'), may hold values from -6 to 6
- key_rows: bfloat16 [12288, 1024], P('ctx', 'heads'), may hold values from -6 to 6
- value_rows: bfloat16 [12288, 1024], P('ctx', 'heads'), may hold values from -6 to 6
Outputs:
- ssm_out: bfloat16 [12288, 8192], P('ctx', 'heads')
- attn_out: bfloat16 [12288, 4096], P('ctx', 'heads')
Inputs may be any that keep to these rules, and one draw needn't show every extreme that they name: `log_decay`: negative everywhere.
All inputs are finite; a program needn't handle non-finite values.
Results may differ from a plain program's by a relative error of at most 0.0075.
Values may be sent and summed in bfloat16 or wider, within the bound.
No kernel may reach another device: no remote copies, remote signals or barrier semaphores. Data moves between devices by JAX's collectives and lax.ppermute only.
A program may use at most 128 MiB of HBM per device.

v0:
```python
import jax
import jax.numpy as jnp
from jax import lax
from jax.sharding import PartitionSpec as P

SSM_HEADS = 128
HEAD_P = 64
STATE = 128
QUERY_HEADS = 32
KV_HEADS = 8
HEAD_DIM = 128
SPAN = 64


def carried_in(part, axis, combine, identity):
    place = lax.axis_index(axis)
    gathered = jax.tree.map(lambda a: lax.all_gather(a, axis), part)
    state = jax.tree.map(lambda a, e: jnp.zeros_like(a) + jnp.asarray(e, a.dtype), part, identity)

    def one(step, state):
        return combine(
            state, jax.tree.map(lambda a: lax.dynamic_index_in_dim(a, step, 0, False), gathered)
        )

    return lax.fori_loop(0, place, one, state)


def chain_combine(earlier, later):
    return (earlier[0] * later[0], later[0][:, None, None] * earlier[1] + later[1])


def local_mixer(ssm_input, gate_input, write_proj, read_proj, log_decay, skip_gain, norm_gain):
    row_count, width_local = ssm_input.shape
    head_local = log_decay.shape[1]
    block_count = row_count // SPAN
    inputs_blk = ssm_input.reshape(block_count, SPAN, head_local, HEAD_P)
    inputs_float = inputs_blk.astype(jnp.float32)
    write_blk = write_proj.reshape(block_count, SPAN, STATE)
    read_blk = read_proj.reshape(block_count, SPAN, STATE)
    cum_decay = jnp.cumsum(log_decay.reshape(block_count, SPAN, head_local), axis=1)
    cum_heads = jnp.transpose(cum_decay, (0, 2, 1))
    causal = jnp.arange(SPAN)[:, None] >= jnp.arange(SPAN)[None, :]
    decay_gap = cum_heads[:, :, :, None] - cum_heads[:, :, None, :]
    decay_mask = jnp.where(causal, jnp.exp(jnp.where(causal, decay_gap, 0.0)), 0.0)
    intersection = jnp.einsum(
        "ctn,csn->cts", read_blk, write_blk, preferred_element_type=jnp.float32
    )
    mix_weights = intersection[:, None] * decay_mask
    y_local = jnp.einsum(
        "chts,cshp->cthp", mix_weights, inputs_float, precision=lax.Precision.HIGHEST
    )
    tail_decay = jnp.exp(cum_heads[:, :, -1:] - cum_heads)
    weighted_write = tail_decay[:, :, :, None] * write_blk[:, None].astype(jnp.float32)
    block_state = jnp.einsum(
        "cshp,chsn->chpn", inputs_float, weighted_write, precision=lax.Precision.HIGHEST
    )
    block_decay = jnp.exp(cum_heads[:, :, -1])

    def prefix_step(carry_in, block_item):
        return (chain_combine(carry_in, block_item), carry_in)

    start_pair = (
        jnp.ones((head_local,), jnp.float32),
        jnp.zeros((head_local, HEAD_P, STATE), jnp.float32),
    )
    device_pair, prefix_pair = lax.scan(prefix_step, start_pair, (block_decay, block_state))
    incoming = carried_in(device_pair, "ctx", chain_combine, start_pair)
    start_state = prefix_pair[0][:, :, None, None] * incoming[1][None] + prefix_pair[1]
    y_carry = (
        jnp.einsum(
            "ctn,chpn->cthp",
            read_blk.astype(jnp.float32),
            start_state,
            precision=lax.Precision.HIGHEST,
        )
        * jnp.exp(cum_decay)[:, :, :, None]
    )
    mixed_out = y_local + y_carry + skip_gain[None, None, :, None] * inputs_float
    gated = mixed_out.reshape(row_count, width_local) * jax.nn.silu(gate_input.astype(jnp.float32))
    square_total = lax.psum(jnp.sum(gated * gated, axis=1), "heads")
    row_scale = lax.rsqrt(square_total / (SSM_HEADS * HEAD_P) + 1e-05)
    return (gated * row_scale[:, None] * norm_gain[None, :]).astype(jnp.bfloat16)


def attend_block(
    state, query_block, query_positions, top_position, key_block, value_block, first_key
):
    scale_factor = 1.0 / HEAD_DIM**0.5
    key_count = key_block.shape[0]

    def compute(state_in):
        running_max, running_sum, running_acc = state_in
        scores = (
            jnp.einsum("gqd,ngd->gqn", query_block, key_block, preferred_element_type=jnp.float32)
            * scale_factor
        )
        key_positions = first_key + jnp.arange(key_count, dtype=jnp.int32)
        visible = key_positions[None, None, :] <= query_positions[None, :, None]
        block_max = jnp.max(jnp.where(visible, scores, -1e30), axis=2)
        new_max = jnp.maximum(running_max, block_max)
        weights = jnp.where(
            visible, jnp.exp(jnp.where(visible, scores - new_max[:, :, None], 0.0)), 0.0
        )
        rescale = jnp.exp(running_max - new_max)
        new_sum = rescale * running_sum + jnp.sum(weights, axis=2)
        new_acc = rescale[:, :, None] * running_acc + jnp.einsum(
            "gqn,ngd->gqd",
            weights.astype(jnp.bfloat16),
            value_block,
            preferred_element_type=jnp.float32,
        )
        return (new_max, new_sum, new_acc)

    return lax.cond(first_key > top_position, lambda state_in: state_in, compute, state)


def attention_local(query_rows, key_rows, value_rows):
    row_count = query_rows.shape[0]
    head_sets = key_rows.shape[1] // HEAD_DIM
    group_size = QUERY_HEADS // KV_HEADS
    own_index = lax.axis_index("ctx")
    query_stack = query_rows.reshape(row_count, head_sets, group_size, HEAD_DIM)
    query_stack = jnp.transpose(query_stack, (1, 0, 2, 3)).reshape(
        head_sets, row_count * group_size, HEAD_DIM
    )
    stacked_rows = jnp.arange(row_count * group_size, dtype=jnp.int32) // group_size
    own_positions = own_index * row_count + stacked_rows
    query_sets = [(query_stack, own_positions)]
    tops = [jnp.max(positions) for _, positions in query_sets]
    carries = tuple(
        (
            (
                jnp.full((head_sets, block.shape[1]), -1e30, jnp.float32),
                jnp.zeros((head_sets, block.shape[1]), jnp.float32),
                jnp.zeros((head_sets, block.shape[1], HEAD_DIM), jnp.float32),
            )
            for block, _ in query_sets
        )
    )
    key_piece = lax.all_gather(key_rows, "ctx", axis=0, tiled=True)
    value_piece = lax.all_gather(value_rows, "ctx", axis=0, tiled=True)
    piece_rows = key_piece.shape[0]
    key_blocks = key_piece.reshape(piece_rows // row_count, row_count, head_sets, HEAD_DIM)
    value_blocks = value_piece.reshape(piece_rows // row_count, row_count, head_sets, HEAD_DIM)
    offsets = row_count * jnp.arange(piece_rows // row_count, dtype=jnp.int32)

    def inner_step(states, block_item):
        key_block, value_block, first_key = block_item
        updated = tuple(
            (
                attend_block(
                    states[number],
                    query_sets[number][0],
                    query_sets[number][1],
                    tops[number],
                    key_block,
                    value_block,
                    first_key,
                )
                for number in range(len(query_sets))
            )
        )
        return (updated, None)

    result, _ = lax.scan(inner_step, carries, (key_blocks, value_blocks, offsets))
    finished = [(state[2] / state[1][:, :, None]).astype(jnp.bfloat16) for state in result]
    combined = finished[0]
    combined = combined.reshape(head_sets, row_count, group_size, HEAD_DIM)
    return jnp.transpose(combined, (1, 0, 2, 3)).reshape(
        row_count, head_sets * group_size * HEAD_DIM
    )


def body(
    ssm_input,
    gate_input,
    write_proj,
    read_proj,
    log_decay,
    skip_gain,
    norm_gain,
    query_rows,
    key_rows,
    value_rows,
):
    ssm_out = local_mixer(
        ssm_input, gate_input, write_proj, read_proj, log_decay, skip_gain, norm_gain
    )
    attn_out = attention_local(query_rows, key_rows, value_rows)
    return (ssm_out, attn_out)


def solution(mesh):
    in_specs = (
        P("ctx", "heads"),
        P("ctx", "heads"),
        P("ctx", None),
        P("ctx", None),
        P("ctx", "heads"),
        P("heads"),
        P("heads"),
        P("ctx", "heads"),
        P("ctx", "heads"),
        P("ctx", "heads"),
    )
    out_specs = (P("ctx", "heads"), P("ctx", "heads"))
    return jax.shard_map(body, mesh=mesh, in_specs=in_specs, out_specs=out_specs, check_vma=False)
```

profile of v0, /device:TPU:63, one launch (start us, length us, event | category | flops | bytes accessed | tf_op | source)
XLA Modules:
  0.0 625.4 jit_solution(15439639091845416310)
XLA Ops:
  13.1 6.8 %while.46 = (s32[]{:T(128)}, f32[16]{0:T(128)S(1)}, f32[16,64,128]{2,1,0:T(8,128)S(1)}, f32[3,16]{1,0:T(4,128)}, f32[3,16,64,128]{3,2,1,0:T(8,128)}, /*index=5*/...) while((s32[]{:T(128)}, f32[16]{0:T(128)S(1)}, ...), condition=%wide.region_2.3_spmd.clone, body=%wide.region_1.2_spmd.clone.sunk | while | flops 524323 | bytes 2622581 | solution.py:66
  23.0 124.2 %all-reduce = f32[1024]{0:T(1024)S(1)} all-reduce(f32[1024]{0:T(1024)S(1)} %dynamic-update-slice), channel_id=2, replica_groups=mesh['ctx'=64,'heads'=8] {'ctx'}, use_global_device_ids=true, to_apply=%add | all-reduce | flops 1024 | bytes 8192
  148.4 33.0 %all-gather.8.cloned.1.call-done = bf16[12288,128]{1,0:T(8,128)(2,1)} async-done(((bf16[192,128]{1,0:T(8,128)(2,1)}), bf16[12288,128]{1,0:T(8,128)(2,1)}) %all-gather.8.cloned.1.call-update) | async-done | bytes 3145744 | tf_op jit(solution)/shard_map/all_gather | solution.py:141
  181.4 336.1 %while.45 = (s32[]{:T(128)}, f32[1,768]{1,0:T(1,128)S(1)}, f32[1,768]{1,0:T(1,128)S(1)}, f32[1,768,128]{2,1,0:T(8,128)S(1)}, s32[64]{0:T(128)S(1)}, /*index=5*/s...) while((s32[]{:T(128)}, f32[1,768]{1,0:T(1,128)S(1)}, ...), condition=%wide.region_13.14_spmd.clone, body=%wide.region_8.13_spmd.clone.sunk | while | flops 77767872 | bytes 2938171 | solution.py:165
  183.4 3.3 conditional.3
  188.6 3.3 conditional.3
  199.1 3.3 conditional.3
  204.4 3.3 conditional.3
  209.6 3.3 conditional.3
  220.1 3.3 conditional.3
  251.6 3.3 conditional.3
  256.9 3.3 conditional.3
  262.1 3.3 conditional.3
  267.4 3.3 conditional.3
  272.7 3.3 conditional.3
  277.9 3.3 conditional.3
  283.2 3.3 conditional.3
  288.5 3.3 conditional.3
  293.7 3.3 conditional.3
  299.0 3.3 conditional.3
  309.5 3.3 conditional.3
  314.7 3.3 conditional.3
  518.6 78.0 %while.44 = (s32[]{:T(128)}, f32[16,64,128]{2,1,0:T(8,128)S(1)}, s32[]{:T(128)}, f32[64,16]{1,0:T(8,128)S(1)}, f32[64,16,64,128]{3,2,1,0:T(8,128)}, /*index=5*/s32[]{:T(128)}, s32[]{:T(128)}, s32[]{:T(128)}) while((s32[]{:T(128)}, f32[16,64,128]{2,1,0:T(8,128)S(1)}, s32[]{:T(128)}, f32[64,16]{1,0:T(8,128)S(1)}, f32[64,16,64,128]{3,2,1,0:T(8,128)}, ...), condition=%wide.region_4.5_spmd, body=%wide.region_3.4_spmd.sunk | while | flops 262149 | bytes 1573183 | solution.py:25
  603.3 14.5 %psum.7 = f32[192]{0:T(256)S(1)} all-reduce(f32[192]{0:T(256)S(1)} %multiply_reduce_fusion), channel_id=1, replica_groups=mesh['ctx'=64,'heads'=8] {'heads'}, use_global_device_ids=true, to_apply=%region_6.7 | all-reduce | flops 192 | bytes 1536 | tf_op jit(solution)/shard_map/psum | solution.py:80
  (952 shorter events, 503.4 us)
Async XLA Ops:
  7.2 141.0 %copy-start = (bf16[192,128]{1,0:T(8,128)(2,1)S(1)}, bf16[192,128]{1,0:T(8,128)(2,1)}, u32[]{:S(2)}) copy-start(bf16[192,128]{1,0:T(8,128)(2,1)} %param.21) | copy-start | bytes 147460
  7.2 4.2 copy-start.5
  7.2 141.2 %all-gather.6.cloned.1.call-start = ((), (), s32[]{:S(2)}) async-start(), calls=%async_computation | async-start | bytes 3194880 | tf_op jit(solution)/shard_map/all_gather | solution.py:140
  7.9 173.5 %all-gather.8.cloned.1.call-start = ((), (), s32[]{:S(2)}) async-start(), calls=%async_computation.1 | async-start | bytes 3194880 | tf_op jit(solution)/shard_map/all_gather | solution.py:141
  8.7 509.9 %all-gather.10.cloned.1.call-start = ((), (), s32[]{:S(2)}) async-start(), calls=%async_computation.2 | async-start | bytes 34078720 | tf_op jit(solution)/shard_map/all_gather | solution.py:17
  13.1 134.2 %copy-start.4 = (bf16[192,512]{1,0:T(8,128)(2,1)S(1)}, bf16[192,512]{1,0:T(8,128)(2,1)}, u32[]{:S(2)}) copy-start(bf16[192,512]{1,0:T(8,128)(2,1)} %param.25) | copy-start | bytes 589828
  20.0 0.8 copy-start.1
  518.6 78.1 %copy-start.2 = (f32[3,16,64,128]{3,2,1,0:T(8,128)S(1)}, f32[3,16,64,128]{3,2,1,0:T(8,128)}, u32[]{:S(2)}) copy-start(f32[3,16,64,128]{3,2,1,0:T(8,128)} %get-tuple-element.226) | copy-start | bytes 4718596
  518.6 78.1 %copy-start.7 = (f32[3,16]{1,0:T(4,128)S(1)}, f32[3,16]{1,0:T(4,128)}, u32[]{:S(2)}) copy-start(f32[3,16]{1,0:T(4,128)} %get-tuple-element.222) | copy-start | bytes 580
  596.7 2.5 copy-start.8
  602.0 1.0 copy-start.3
  602.0 15.8 %copy-start.6 = (f32[1024]{0:T(1024)S(1)}, f32[1024]{0:T(1024)}, u32[]{:S(2)}) copy-start(f32[1024]{0:T(1024)} %param.24) | copy-start | bytes 12292
Sparse Core Ops, SparseCore 0:
  11.4 85.3 all-gather.5
  100.1 81.2 all-gather.7
  184.8 144.7 all-gather.9
where the time goes:
time: 637 us; the launch traced here: 625 us
  matrix products  157 us (25%)
  blocking collectives  139 us (22%)
  other arithmetic  138 us (22%)
  loops' own time  88.4 us (14%)
  local copies, waits for them, and re-layouts  54.1 us (8%)
  waiting for transfers between devices  34.4 us (5%)
  between operations  14.7 us (2%)
    unnamed x1, blocking collectives  124 us
    dot_general x64, matrix products, compute(): jnp.einsum('gqn,ngd->gqd', weights.astype(jnp.bfloat16), value_block, pre...  83.3 us
    another operation x1, loops' own time, attention_local(): lax.scan(inner_step, carries, (key_blocks, value_blocks, offsets))  81.8 us
    add x66, other arithmetic, chain_combine(): later[0][:, None, None] * earlier[1] + later[1]  75.3 us
    dot_general x64, matrix products, compute(): jnp.einsum('gqd,ngd->gqn', query_block, key_block, preferred_element_type...  68.2 us
    dynamic_slice x64, local copies, waits for them, and re-layouts, attention_local(): lax.scan(inner_step, carries, (key_blocks, value_blocks, offsets))  41.2 us
    add x64, other arithmetic, compute(): key_positions = first_key + jnp.arange(key_count, dtype=jnp.int32)  39.9 us
    all_gather x1, waiting for transfers between devices, attention_local(): value_piece = lax.all_gather(value_rows, 'ctx', axis=0, tiled=True)  33 us
  transfers between devices with their start and end apart: 3, of which 1 were waited for; matrix products, arithmetic and copies ran while one was open for 42% of the time, Pallas kernels for 0%

commit v1 on v0

--- a/solution.py
+++ b/solution.py
@@ -138,7 +138,9 @@
         )
     )
     key_piece = lax.all_gather(key_rows, "ctx", axis=0, tiled=True)
-    value_piece = lax.all_gather(value_rows, "ctx", axis=0, tiled=True)
+    value_piece = jnp.concatenate(
+        lax.all_to_all(jnp.stack([value_rows] * lax.axis_size("ctx")), "ctx", 0, 0), axis=0
+    )
     piece_rows = key_piece.shape[0]
     key_blocks = key_piece.reshape(piece_rows // row_count, row_count, head_sets, HEAD_DIM)
     value_blocks = value_piece.reshape(piece_rows // row_count, row_count, head_sets, HEAD_DIM)

time: 637 us -> 681 us (1.069)
  blocking collectives: 139 us -> 209 us
  waiting for transfers between devices: 34.4 us -> 0.72 us
  starting transfers between devices: 0.11 us -> 10.9 us
    unnamed x1, blocking collectives: 124 us -> 190 us
    all_gather x1 -> x0, waiting for transfers between devices: 33 us -> none  [attention_local(): value_piece = lax.all_gather(value_rows, 'ctx', axis=0, tiled=True)]
    all_to_all x0 -> x1, starting transfers between devices: none -> 10.9 us  [attention_local(): lax.all_to_all(jnp.stack([value_rows] * lax.axis_size('ctx')), 'ctx', 0, 0)]
  transfers between devices with their start and end apart: 3 -> 3, of which waited for: 1 -> 0; matrix products, arithmetic and copies ran while one was open for 42% -> 39% of each run, Pallas kernels for 0% -> 0%
where the time goes in v1:
time: 681 us; the launch traced here: 669 us
  blocking collectives  209 us (31%)
  matrix products  157 us (23%)
  other arithmetic  137 us (20%)
  loops' own time  88.7 us (13%)
  local copies, waits for them, and re-layouts  49.9 us (7%)
  between operations  15 us (2%)
  starting transfers between devices  10.9 us (2%)
    unnamed x1, blocking collectives  190 us
    dot_general x64, matrix products, compute(): jnp.einsum('gqn,ngd->gqd', weights.astype(jnp.bfloat16), value_block, pre...  83.2 us
    another operation x1, loops' own time, attention_local(): lax.scan(inner_step, carries, (key_blocks, value_blocks, offsets))  82.1 us
    add x66, other arithmetic, chain_combine(): later[0][:, None, None] * earlier[1] + later[1]  75.3 us
    dot_general x64, matrix products, compute(): jnp.einsum('gqd,ngd->gqn', query_block, key_block, preferred_element_type...  68.4 us
    add x64, other arithmetic, compute(): key_positions = first_key + jnp.arange(key_count, dtype=jnp.int32)  39.6 us
    dynamic_slice x64, local copies, waits for them, and re-layouts, attention_local(): lax.scan(inner_step, carries, (key_blocks, value_blocks, offsets))  38.1 us
    psum x1, blocking collectives, local_mixer(): square_total = lax.psum(jnp.sum(gated * gated, axis=1), 'heads')  19.3 us
  transfers between devices with their start and end apart: 3, of which 0 were waited for; matrix products, arithmetic and copies ran while one was open for 39% of the time, Pallas kernels for 0%

profile of v1, /device:TPU:63, one launch (start us, length us, event | category | flops | bytes accessed | tf_op | source)
XLA Modules:
  0.0 669.4 jit_solution(1923696052921374125)
XLA Ops:
  18.8 10.9 %all-to-all-start = ((bf16[64,192,128]{2,1,0:T(8,128)(2,1)}), bf16[64,192,128]{2,1,0:T(8,128)(2,1)}, u32[]{:S(2)}, u32[]{:S(2)}) async-start(bf16[64,192,128]{2,1,0:T(8,128)(2,1)} %stack.2), calls=%async_computation | async-start | bytes 6291456 | tf_op jit(solution)/shard_map/all_to_all | solution.py:142
  31.9 190.1 %all-reduce = f32[1024]{0:T(1024)S(1)} all-reduce(f32[1024]{0:T(1024)S(1)} %dynamic-update-slice), channel_id=2, replica_groups=mesh['ctx'=64,'heads'=8] {'ctx'}, use_global_device_ids=true, to_apply=%add | all-reduce | flops 1024 | bytes 8192
  223.2 333.1 %while.45 = (s32[]{:T(128)}, f32[1,768]{1,0:T(1,128)S(1)}, f32[1,768]{1,0:T(1,128)S(1)}, f32[1,768,128]{2,1,0:T(8,128)S(1)}, s32[64]{0:T(128)S(1)}, /*index=5*/s...) while((s32[]{:T(128)}, f32[1,768]{1,0:T(1,128)S(1)}, ...), condition=%wide.region_13.14_spmd.clone, body=%wide.region_8.13_spmd.clone.sunk | while | flops 77767872 | bytes 2938171 | solution.py:167
  230.3 3.3 conditional.3
  240.7 3.3 conditional.3
  251.1 3.3 conditional.3
  261.6 3.3 conditional.3
  277.2 3.3 conditional.3
  292.8 3.3 conditional.3
  308.4 3.3 conditional.3
  324.0 3.3 conditional.3
  339.6 3.3 conditional.3
  355.2 3.3 conditional.3
  386.5 3.3 conditional.3
  402.1 3.3 conditional.3
  417.7 3.3 conditional.3
  433.3 3.3 conditional.3
  448.9 3.3 conditional.3
  464.5 3.3 conditional.3
  480.1 3.3 conditional.3
  495.8 3.3 conditional.3
  511.4 3.3 conditional.3
  557.4 78.2 %while.44 = (s32[]{:T(128)}, f32[16,64,128]{2,1,0:T(8,128)S(1)}, s32[]{:T(128)}, f32[64,16]{1,0:T(8,128)S(1)}, f32[64,16,64,128]{3,2,1,0:T(8,128)}, /*index=5*/s32[]{:T(128)}, s32[]{:T(128)}, s32[]{:T(128)}) while((s32[]{:T(128)}, f32[16,64,128]{2,1,0:T(8,128)S(1)}, s32[]{:T(128)}, f32[64,16]{1,0:T(8,128)S(1)}, f32[64,16,64,128]{3,2,1,0:T(8,128)}, ...), condition=%wide.region_4.5_spmd, body=%wide.region_3.4_spmd.sunk | while | flops 262149 | bytes 1573183 | solution.py:25
  642.2 19.3 %psum.7 = f32[192]{0:T(256)S(1)} all-reduce(f32[192]{0:T(256)S(1)} %multiply_reduce_fusion), channel_id=1, replica_groups=mesh['ctx'=64,'heads'=8] {'heads'}, use_global_device_ids=true, to_apply=%region_6.7 | all-reduce | flops 192 | bytes 1536 | tf_op jit(solution)/shard_map/psum | solution.py:80
  (952 shorter events, 497.9 us)
Async XLA Ops:
  7.2 215.8 %copy-start = (bf16[192,128]{1,0:T(8,128)(2,1)S(1)}, bf16[192,128]{1,0:T(8,128)(2,1)}, u32[]{:S(2)}) copy-start(bf16[192,128]{1,0:T(8,128)(2,1)} %param.21) | copy-start | bytes 147460
  7.2 3.5 copy-start.5
  7.2 216.0 %all-gather.5.cloned.1.call-start = ((), (), s32[]{:S(2)}) async-start(), calls=%async_computation.1 | async-start | bytes 3194880 | tf_op jit(solution)/shard_map/all_gather | solution.py:140
  7.9 549.4 %all-gather.7.cloned.1.call-start = ((), (), s32[]{:S(2)}) async-start(), calls=%async_computation.2 | async-start | bytes 34078720 | tf_op jit(solution)/shard_map/all_gather | solution.py:17
  12.4 4.0 copy-start.6
  15.5 0.8 copy-start.1
  18.8 203.3 %copy-start.4 = (bf16[192,512]{1,0:T(8,128)(2,1)S(1)}, bf16[192,512]{1,0:T(8,128)(2,1)}, u32[]{:S(2)}) copy-start(bf16[192,512]{1,0:T(8,128)(2,1)} %param.25) | copy-start | bytes 589828
  18.8 204.3 %all-to-all-start = ((bf16[64,192,128]{2,1,0:T(8,128)(2,1)}), bf16[64,192,128]{2,1,0:T(8,128)(2,1)}, u32[]{:S(2)}, u32[]{:S(2)}) async-start(bf16[64,192,128]{2,1,0:T(8,128)(2,1)} %stack.2), calls=%async_computation | async-start | bytes 6291456 | tf_op jit(solution)/shard_map/all_to_all | solution.py:142
  557.4 78.2 %copy-start.2 = (f32[3,16,64,128]{3,2,1,0:T(8,128)S(1)}, f32[3,16,64,128]{3,2,1,0:T(8,128)}, u32[]{:S(2)}) copy-start(f32[3,16,64,128]{3,2,1,0:T(8,128)} %get-tuple-element.226) | copy-start | bytes 4718596
  635.6 2.5 copy-start.8
  640.9 1.0 copy-start.3
  640.9 20.6 %copy-start.7 = (f32[1024]{0:T(1024)S(1)}, f32[1024]{0:T(1024)}, u32[]{:S(2)}) copy-start(f32[1024]{0:T(1024)} %param.24) | copy-start | bytes 12292
Sparse Core Ops, SparseCore 0:
  11.4 96.7 all-gather.4
  111.6 145.4 all-gather.6
